TPU v7x, 32 devices: a whole 2x2x4 slice. The times are simulated.
32 devices in a mesh: fsdp: 8 (over z, x), ckpt: 4 (over y, core).
Axes of the slice: x: 2, y: 2, z: 4, core: 2. Of those that a mesh axis runs over, the one named last changes fastest.
Arguments:
- act_table: bfloat16 [4, 2048, 4096], P('ckpt', 'fsdp'), may hold values from -6 to 6
- token_ids: int32 [4, 2048], P('ckpt'), may hold values from 0 to 2047, each once within a row
- lengths: int32 [4, 8], P('ckpt'), may hold values from 1 to 384, 2048 in all within a row
- grads: bfloat16 [4, 2048, 14336], P('ckpt', 'fsdp'), may hold values from -0.19921875 to 0.19921875
- weights: bfloat16 [4, 8, 4096, 1792], P('ckpt', 'fsdp'), may hold values from -6 to 6
Outputs:
- merged: bfloat16 [8, 4096, 1792], P('fsdp', 'ckpt')
- merge_weight: float32 [8, 4096, 1792], P('fsdp', 'ckpt')
Inputs may be any that keep to these rules, and one draw needn't show every extreme that they name: `token_ids`: each checkpoint's row names every row of the activation table once. One checkpoint's lengths sum to 2048, and one of them is exactly 384.
All inputs are finite; a program needn't handle non-finite values.
Results may differ from a plain program's by a relative error of at most 0.001.
Values may be sent and summed in bfloat16 or wider, within the bound.
No kernel may reach another device: no remote copies, remote signals or barrier semaphores. Data moves between devices by JAX's collectives and lax.ppermute only.
A program may use at most 256 MiB of HBM per device.

v0:
```python
import jax
import jax.numpy as jnp
from jax import lax
from jax.sharding import PartitionSpec as P

NCB = 8
MOST = 384
prior_mass = 0.1


def example_fisher(act_rows, grad_rows, example_lengths, longest):
    row_starts = jnp.cumsum(example_lengths) - example_lengths
    padded_rows = jnp.concatenate(
        [act_rows, jnp.zeros((longest, act_rows.shape[1]), act_rows.dtype)], 0
    )
    padded_grads = jnp.concatenate(
        [grad_rows, jnp.zeros((longest, grad_rows.shape[1]), grad_rows.dtype)], 0
    )
    positions = jnp.arange(longest, dtype=jnp.int32)

    def add_example(example, running):
        row_start = row_starts[example]
        act_block = lax.dynamic_slice_in_dim(padded_rows, row_start, longest, 0)
        keep = (positions < example_lengths[example])[:, None]
        act_block = jnp.where(keep, act_block, jnp.zeros_like(act_block))
        grad_block = lax.dynamic_slice_in_dim(padded_grads, row_start, longest, 0)
        example_grad = lax.dot_general(
            act_block, grad_block, (((0,), (0,)), ((), ())), preferred_element_type=jnp.float32
        )
        return running + example_grad * example_grad

    start_value = jnp.zeros((act_rows.shape[1], grad_rows.shape[1]), jnp.float32)
    return lax.fori_loop(0, example_lengths.shape[0], add_example, start_value)


def body(act_table, token_ids, lengths, grads, weights):
    group_width = lax.axis_size("fsdp")
    row_blocks = group_width // NCB
    own_rows = act_table[0]
    local_count = own_rows.shape[0]
    feature_width = own_rows.shape[1] // row_blocks
    act_parts = jnp.broadcast_to(
        own_rows.reshape(local_count, row_blocks, 1, feature_width),
        (local_count, row_blocks, NCB, feature_width),
    )
    act_parts = act_parts.reshape(local_count, group_width * feature_width)
    table_rows = lax.all_to_all(act_parts, "fsdp", split_axis=1, concat_axis=0, tiled=True)
    act_rows = table_rows[token_ids[0]]
    own_grads = grads[0]
    grad_width = own_grads.shape[1]
    grad_parts = jnp.broadcast_to(
        own_grads.reshape(local_count, 1, grad_width), (local_count, row_blocks, grad_width)
    )
    grad_parts = grad_parts.reshape(local_count, row_blocks * grad_width)
    grad_rows = lax.all_to_all(grad_parts, "fsdp", split_axis=1, concat_axis=0, tiled=True)
    fisher = example_fisher(act_rows, grad_rows, lengths[0], MOST)
    fisher_mass = fisher + prior_mass
    own_weight = weights[0, 0]
    group_size = lax.axis_size("ckpt")
    weight_parts = lax.all_to_all(own_weight[None], "ckpt", split_axis=1, concat_axis=0, tiled=True)
    mass_parts = lax.all_to_all(fisher_mass[None], "ckpt", split_axis=1, concat_axis=0, tiled=True)
    numerator = jnp.sum(mass_parts * weight_parts.astype(jnp.float32), axis=0)
    denominator = jnp.sum(mass_parts, axis=0)
    return ((numerator / denominator).astype(jnp.bfloat16)[None], (denominator / group_size)[None])


def solution(mesh):
    placed = (
        P("ckpt", "fsdp", None),
        P("ckpt", None),
        P("ckpt", None),
        P("ckpt", "fsdp", None),
        P("ckpt", "fsdp", None, None),
    )
    return jax.shard_map(
        body,
        mesh=mesh,
        in_specs=placed,
        out_specs=(P("fsdp", "ckpt", None), P("fsdp", "ckpt", None)),
        check_vma=False,
    )
```

profile of v0, /device:TPU:0, one launch (start us, length us, event | category | flops | bytes accessed | tf_op | source)
XLA Modules:
  0.0 1270.1 jit_solution(4994978410783531105)
XLA Ops:
  0.6 8.2 copy.14
  8.9 4.6 copy.10
  13.5 167.8 %all_to_all.56 = bf16[256,8,1792]{2,0,1:T(8,128)(2,1)} all-to-all(bf16[256,8,1792]{2,0,1:T(8,128)(2,1)S(1)} %copy.10), channel_id=1, replica_groups=mesh['fsdp'=8,'ckpt'=4] {'fsdp'}, dimensions={1} | all-to-all | bytes 14680064 | tf_op jit(solution)/shard_map/all_to_all | solution.py:55
  181.3 6.0 broadcast_in_dim.40
  187.2 6.1 all-to-all-start
  193.5 26.1 %copy.16 = bf16[1,4096,1792]{2,0,1:T(2,128)(2,1)} copy(bf16[1,4096,1792]{2,1,0:T(8,128)(2,1)} %bitcast.41) | data formatting | bytes 29360128 | tf_op jit(solution)/shard_map/broadcast_in_dim;squeeze | solution.py:60
  220.1 147.2 %reduce = bf16[4096,1792]{1,0:T(8,128)(2,1)} reduce(bf16[4096,1,1792]{2,1,0:T(2,128)(2,1)} %bitcast.38, bf16[]{:T(256)} %broadcast.59), dimensions={1}, to_apply=%bitcast.30.reduce_sub_computation | reduce | bytes 29360130
  367.4 11.5 reshape.122
  378.9 7.0 concatenate.7
  385.9 169.2 %all-to-all-done = bf16[256,8,4096]{2,0,1:T(8,128)(2,1)} async-done(((bf16[256,8,4096]{2,0,1:T(8,128)(2,1)}), bf16[256,8,4096]{2,0,1:T(8,128)(2,1)}, u32[]{:S(2)}, u32[]{:S(2)}) %all-to-all-start) | async-done | bytes 16777248 | tf_op jit(solution)/shard_map/all_to_all | solution.py:47
  555.1 7.0 all-to-all-start.3
  562.1 36.6 %gather_fusion = bf16[2048,4096]{1,0:T(8,128)(2,1)} fusion(bf16[2048,4096]{1,0:T(8,128)(2,1)} %bitcast.5, s32[2048]{0:T(1024)S(1)} %broadcast_clamp_fusion), kind=kCustom, calls=%fused_computation | custom fusion | bytes 33562624 | tf_op jit(solution)/shard_map/gather | solution.py:48
  598.7 17.6 %concatenate.6 = bf16[2432,4096]{1,0:T(8,128)(2,1)} pad(bf16[2048,4096]{1,0:T(8,128)(2,1)} %gather_fusion, bf16[]{:T(256)} %constant.50.clone.1), padding=0_384x0_0 | pad | bytes 36700160 | tf_op jit(solution)/shard_map/concatenate | solution.py:13
  616.2 221.3 %while.14 = (s32[]{:T(128)}, f32[4096,1792]{1,0:T(8,128)}, s32[8]{0:T(128)S(1)}, s32[8]{0:T(128)S(1)}, bf16[2432,4096]{1,0:T(8,128)(2,1)}, /*index=5*/bf16[2432,1792]{1,0:T(8,128)(2,1)}, s32[]{:T(128)}, s32[]{:T(128)}, s32[]{:T(128)}) while((s32[]{:T(128)}, f32[4096,1792]{1,0:T(8,128)}, s32[8]{0:T(128)S(1)}, s32[8]{0:T(128)S(1)}, ...), condition=%wide.region_2.3_spmd.clone, body=%wide.region_1.2_spmd.clone.sunk | while | flops 5660738048 | bytes 63244708 | solution.py:33
  616.2 0.6 dynamic_slice.44
  618.7 0.6 dynamic_slice.45
  619.3 0.6 iota_compare_fusion.2
  620.0 15.1 %select_add_fusion.2 = f32[4096,1792]{1,0:T(8,128)} fusion(f32[4096,1792]{1,0:T(8,128)} %get-tuple-element.213, pred[]{:T(512)S(6)} %compare.5, bf16[2432,4096]{1,0:T(8,128)(2,1)} %get-tuple-element.225, s32[]{:T(128)S(6)} %select_n.41, pred[384]{0:T(512)(128)(4,1)S(1)} %iota_compare_fusion.2, bf16[2432,1792]{1,0:T(8,128)(2,1)} %get-tuple-element.226), kind=kOutput, calls=%fused_computation.2.clone.1 | convolution fusion | flops 5660737536 | bytes 63244160 | tf_op jit(solution)/shard_map/while/body/eval_jaxpr/dot_general | solution.py:27
  637.6 0.6 dynamic_slice.45
  638.2 0.6 iota_compare_fusion.2
  638.9 25.1 %select_add_fusion.2 = f32[4096,1792]{1,0:T(8,128)} fusion(f32[4096,1792]{1,0:T(8,128)} %get-tuple-element.213, pred[]{:T(512)S(6)} %compare.5, bf16[2432,4096]{1,0:T(8,128)(2,1)} %get-tuple-element.225, s32[]{:T(128)S(6)} %select_n.41, pred[384]{0:T(512)(128)(4,1)S(1)} %iota_compare_fusion.2, bf16[2432,1792]{1,0:T(8,128)(2,1)} %get-tuple-element.226), kind=kOutput, calls=%fused_computation.2.clone.1 | convolution fusion | flops 5660737536 | bytes 63244160 | tf_op jit(solution)/shard_map/while/body/eval_jaxpr/dot_general | solution.py:27
  666.5 0.6 dynamic_slice.45
  667.1 0.6 iota_compare_fusion.2
  667.8 25.1 %select_add_fusion.2 = f32[4096,1792]{1,0:T(8,128)} fusion(f32[4096,1792]{1,0:T(8,128)} %get-tuple-element.213, pred[]{:T(512)S(6)} %compare.5, bf16[2432,4096]{1,0:T(8,128)(2,1)} %get-tuple-element.225, s32[]{:T(128)S(6)} %select_n.41, pred[384]{0:T(512)(128)(4,1)S(1)} %iota_compare_fusion.2, bf16[2432,1792]{1,0:T(8,128)(2,1)} %get-tuple-element.226), kind=kOutput, calls=%fused_computation.2.clone.1 | convolution fusion | flops 5660737536 | bytes 63244160 | tf_op jit(solution)/shard_map/while/body/eval_jaxpr/dot_general | solution.py:27
  695.4 0.6 dynamic_slice.45
  696.0 0.6 iota_compare_fusion.2
  696.7 25.1 %select_add_fusion.2 = f32[4096,1792]{1,0:T(8,128)} fusion(f32[4096,1792]{1,0:T(8,128)} %get-tuple-element.213, pred[]{:T(512)S(6)} %compare.5, bf16[2432,4096]{1,0:T(8,128)(2,1)} %get-tuple-element.225, s32[]{:T(128)S(6)} %select_n.41, pred[384]{0:T(512)(128)(4,1)S(1)} %iota_compare_fusion.2, bf16[2432,1792]{1,0:T(8,128)(2,1)} %get-tuple-element.226), kind=kOutput, calls=%fused_computation.2.clone.1 | convolution fusion | flops 5660737536 | bytes 63244160 | tf_op jit(solution)/shard_map/while/body/eval_jaxpr/dot_general | solution.py:27
  724.3 0.6 dynamic_slice.45
  724.9 0.6 iota_compare_fusion.2
  725.6 25.1 %select_add_fusion.2 = f32[4096,1792]{1,0:T(8,128)} fusion(f32[4096,1792]{1,0:T(8,128)} %get-tuple-element.213, pred[]{:T(512)S(6)} %compare.5, bf16[2432,4096]{1,0:T(8,128)(2,1)} %get-tuple-element.225, s32[]{:T(128)S(6)} %select_n.41, pred[384]{0:T(512)(128)(4,1)S(1)} %iota_compare_fusion.2, bf16[2432,1792]{1,0:T(8,128)(2,1)} %get-tuple-element.226), kind=kOutput, calls=%fused_computation.2.clone.1 | convolution fusion | flops 5660737536 | bytes 63244160 | tf_op jit(solution)/shard_map/while/body/eval_jaxpr/dot_general | solution.py:27
  753.2 0.6 dynamic_slice.45
  753.8 0.6 iota_compare_fusion.2
  754.5 25.1 %select_add_fusion.2 = f32[4096,1792]{1,0:T(8,128)} fusion(f32[4096,1792]{1,0:T(8,128)} %get-tuple-element.213, pred[]{:T(512)S(6)} %compare.5, bf16[2432,4096]{1,0:T(8,128)(2,1)} %get-tuple-element.225, s32[]{:T(128)S(6)} %select_n.41, pred[384]{0:T(512)(128)(4,1)S(1)} %iota_compare_fusion.2, bf16[2432,1792]{1,0:T(8,128)(2,1)} %get-tuple-element.226), kind=kOutput, calls=%fused_computation.2.clone.1 | convolution fusion | flops 5660737536 | bytes 63244160 | tf_op jit(solution)/shard_map/while/body/eval_jaxpr/dot_general | solution.py:27
  782.1 0.6 dynamic_slice.45
  782.7 0.6 iota_compare_fusion.2
  783.4 25.2 %select_add_fusion.2 = f32[4096,1792]{1,0:T(8,128)} fusion(f32[4096,1792]{1,0:T(8,128)} %get-tuple-element.213, pred[]{:T(512)S(6)} %compare.5, bf16[2432,4096]{1,0:T(8,128)(2,1)} %get-tuple-element.225, s32[]{:T(128)S(6)} %select_n.41, pred[384]{0:T(512)(128)(4,1)S(1)} %iota_compare_fusion.2, bf16[2432,1792]{1,0:T(8,128)(2,1)} %get-tuple-element.226), kind=kOutput, calls=%fused_computation.2.clone.1 | convolution fusion | flops 5660737536 | bytes 63244160 | tf_op jit(solution)/shard_map/while/body/eval_jaxpr/dot_general | solution.py:27
  811.1 0.6 dynamic_slice.45
  811.7 0.6 iota_compare_fusion.2
  812.4 25.1 %select_add_fusion.2 = f32[4096,1792]{1,0:T(8,128)} fusion(f32[4096,1792]{1,0:T(8,128)} %get-tuple-element.213, pred[]{:T(512)S(6)} %compare.5, bf16[2432,4096]{1,0:T(8,128)(2,1)} %get-tuple-element.225, s32[]{:T(128)S(6)} %select_n.41, pred[384]{0:T(512)(128)(4,1)S(1)} %iota_compare_fusion.2, bf16[2432,1792]{1,0:T(8,128)(2,1)} %get-tuple-element.226), kind=kOutput, calls=%fused_computation.2.clone.1 | convolution fusion | flops 5660737536 | bytes 63244160 | tf_op jit(solution)/shard_map/while/body/eval_jaxpr/dot_general | solution.py:27
  837.5 21.6 %broadcast_add_fusion = f32[4096,1792]{1,0:T(8,128)} fusion(f32[4096,1792]{1,0:T(8,128)} %get-tuple-element.126), kind=kLoop, calls=%fused_computation.12 | loop fusion | flops 7340032 | bytes 58720256 | tf_op jit(solution)/shard_map/add | solution.py:57
  859.1 24.0 %broadcast_in_dim.41 = f32[1,4096,1792]{2,0,1:T(1,128)} reshape(f32[4096,1792]{1,0:T(8,128)} %broadcast_add_fusion) | data formatting | bytes 58720256 | tf_op jit(solution)/shard_map/broadcast_in_dim | solution.py:61
  883.0 9.4 all-to-all-start.2
  892.4 32.2 %reshape.123 = bf16[4096,1,1792]{2,1,0:T(2,128)(2,1)} reshape(bf16[4,2,917504]{2,1,0:T(2,128)(2,1)} %all-to-all-done.3) | data formatting | bytes 29360128
  924.7 23.8 %copy.13 = f32[1,4096,1792]{2,1,0:T(8,128)} copy(bf16[1,4096,1792]{2,0,1:T(2,128)(2,1)} %bitcast.37) | data formatting | bytes 44040192
  948.5 261.5 %all-to-all-done.2 = f32[1,4096,1792]{2,0,1:T(1,128)} async-done(((f32[1,4096,1792]{2,0,1:T(1,128)}), f32[1,4096,1792]{2,0,1:T(1,128)}, u32[]{:S(2)}, u32[]{:S(2)}) %all-to-all-start.2) | async-done | bytes 29360160 | tf_op jit(solution)/shard_map/all_to_all | solution.py:61
  1210.0 23.9 %copy.12 = f32[1,4096,1792]{2,1,0:T(8,128)} copy(f32[1,4096,1792]{2,0,1:T(1,128)} %all-to-all-done.2) | data formatting | bytes 58720256
  1233.9 25.5 %fusion.10 = (f32[1024,1792]{1,0:T(8,128)}, f32[1024,1792]{1,0:T(8,128)}) fusion(f32[4,1024,1792]{2,1,0:T(8,128)} %bitcast.36, f32[4,1024,1792]{2,1,0:T(8,128)} %bitcast.35), kind=kLoop, calls=%fused_computation.19 | loop fusion | flops 18350080 | bytes 73400320 | tf_op jit(solution)/shard_map/reduce_sum | solution.py:63
  1259.4 10.7 multiply_bitcast_fusion
  (20 shorter events, 4.8 us)
Async XLA Ops:
  8.9 172.4 %copy-start = (bf16[1,256,4096]{2,1,0:T(8,128)(2,1)S(1)}, bf16[1,256,4096]{2,1,0:T(8,128)(2,1)}, u32[]{:S(2)}) copy-start(bf16[1,256,4096]{2,1,0:T(8,128)(2,1)} %param.7) | copy-start | bytes 6291460
  187.2 6.1 copy-start.2
  187.2 367.8 %all-to-all-start = ((bf16[256,8,4096]{2,0,1:T(8,128)(2,1)}), bf16[256,8,4096]{2,0,1:T(8,128)(2,1)}, u32[]{:S(2)}, u32[]{:S(2)}) async-start(bf16[256,8,4096]{2,0,1:T(8,128)(2,1)} %broadcast_in_dim.40), calls=%async_computation | async-start | bytes 33554432 | tf_op jit(solution)/shard_map/all_to_all | solution.py:47
  367.4 11.5 copy-start.1
  555.1 328.0 %all-to-all-start.3 = ((bf16[4,2,917504]{2,1,0:T(2,128)(2,1)}), bf16[4,2,917504]{2,1,0:T(2,128)(2,1)}, u32[]{:S(2)}, u32[]{:S(2)}) async-start(bf16[4,2,917504]{2,1,0:T(2,128)(2,1)} %reshape.122), calls=%async_computation.3 | async-start | bytes 29360128 | tf_op jit(solution)/shard_map/all_to_all | solution.py:60
  883.0 327.0 %all-to-all-start.2 = ((f32[1,4096,1792]{2,0,1:T(1,128)}), f32[1,4096,1792]{2,0,1:T(1,128)}, u32[]{:S(2)}, u32[]{:S(2)}) async-start(f32[1,4096,1792]{2,0,1:T(1,128)} %broadcast_in_dim.41), calls=%async_computation.2 | async-start | bytes 58720256 | tf_op jit(solution)/shard_map/all_to_all | solution.py:61
where the time goes:
time: 1270 us
  waiting for transfers between devices  431 us (34%)
  local copies, waits for them, and re-layouts  231 us (18%)
  other arithmetic  210 us (17%)
  matrix products  191 us (15%)
  blocking collectives  168 us (13%)
  starting transfers between devices  22.5 us (2%)
  loops' own time  15.7 us (1%)
    all_to_all x1, waiting for transfers between devices, body(): lax.all_to_all(fisher_mass[None], 'ckpt', split_axis=1, concat_axis=0, ti...  262 us
    dot_general x8, matrix products, add_example(): lax.dot_general(act_block, grad_block, (((0,), (0,)), ((), ())), preferre...  191 us
    all_to_all x1, waiting for transfers between devices, body(): lax.all_to_all(act_parts, 'fsdp', split_axis=1, concat_axis=0, tiled=True)  169 us
    all_to_all x1, blocking collectives, body(): lax.all_to_all(grad_parts, 'fsdp', split_axis=1, concat_axis=0, tiled=True)  168 us
    unnamed x2, other arithmetic  147 us
    unnamed x12, local copies, waits for them, and re-layouts  100 us
    gather x1, local copies, waits for them, and re-layouts, body(): act_rows = table_rows[token_ids[0]]  36.6 us
    another operation x1, local copies, waits for them, and re-layouts, body(): own_weight[None]  26.1 us
  transfers between devices with their start and end apart: 3, of which 2 were waited for; matrix products, arithmetic and copies ran while one was open for 44% of the time, Pallas kernels for 0%

commit v1 on v0

--- a/solution.py
+++ b/solution.py
@@ -1,11 +1,41 @@
+import functools
 import jax
 import jax.numpy as jnp
 from jax import lax
 from jax.sharding import PartitionSpec as P
+from jax.lax import axis_index, axis_size, ppermute
 
 NCB = 8
 MOST = 384
 prior_mass = 0.1
+
+
+def switch_local_data_in(local_block, where_dim, slab_in):
+    w_next, arr_out = (local_block.shape[:where_dim], local_block.shape[where_dim + 1 :])
+    return jnp.moveaxis(local_block.reshape(*w_next, slab_in, -1, *arr_out), where_dim, 0)
+
+
+def point_serve(xx, row_dim):
+    xx = jnp.moveaxis(xx, 0, row_dim)
+    ready = xx.shape
+    return xx.reshape(*ready[:row_dim], ready[row_dim] * ready[row_dim + 1], *ready[row_dim + 2 :])
+
+
+def write_samples(tile_in, mesh_ax, x_in, q_in):
+    current_arr, heard = (axis_size(mesh_ax), axis_index(mesh_ax))
+    extra = switch_local_data_in(tile_in, q_in, current_arr)
+    odd = extra
+    for pp in range(1, current_arr):
+        tmp, current_value = ((heard + pp) % current_arr, (heard - pp) % current_arr)
+        u_next = lax.dynamic_index_in_dim(extra, tmp, 0)
+        o_now = ppermute(
+            u_next, mesh_ax, perm=[(no, (no + pp) % current_arr) for no in range(current_arr)]
+        )
+        odd = lax.dynamic_update_slice_in_dim(odd, o_now, current_value, axis=0)
+    return point_serve(odd, x_in)
+
+
+return_all_the_groups = functools.partial(write_samples, mesh_ax="fsdp", x_in=0, q_in=1)
 
 
 def example_fisher(act_rows, grad_rows, example_lengths, longest):
@@ -44,7 +74,7 @@
         (local_count, row_blocks, NCB, feature_width),
     )
     act_parts = act_parts.reshape(local_count, group_width * feature_width)
-    table_rows = lax.all_to_all(act_parts, "fsdp", split_axis=1, concat_axis=0, tiled=True)
+    table_rows = return_all_the_groups(act_parts)
     act_rows = table_rows[token_ids[0]]
     own_grads = grads[0]
     grad_width = own_grads.shape[1]

time: 1270 us -> 1270 us (level)
  the two profiles are of different devices: /device:TPU:0 before, /device:TPU:26 now
where the time goes in v1:
time: 1270 us; the launch traced here: 1260 us
  waiting for transfers between devices  565 us (44%)
  local copies, waits for them, and re-layouts  247 us (19%)
  other arithmetic  210 us (17%)
  matrix products  191 us (15%)
  starting transfers between devices  35.4 us (3%)
  loops' own time  15.7 us (1%)
    ppermute x7, waiting for transfers between devices, write_samples(): ppermute(u_next, mesh_ax, perm=[(no, (no + pp) % current_arr) for no in r...  304 us
    all_to_all x1, waiting for transfers between devices, body(): lax.all_to_all(fisher_mass[None], 'ckpt', split_axis=1, concat_axis=0, ti...  262 us
    dot_general x8, matrix products, add_example(): lax.dot_general(act_block, grad_block, (((0,), (0,)), ((), ())), preferre...  191 us
    unnamed x2, other arithmetic  147 us
    unnamed x12, local copies, waits for them, and re-layouts  97.1 us
    gather x1, local copies, waits for them, and re-layouts, body(): act_rows = table_rows[token_ids[0]]  36.5 us
    another operation x1, local copies, waits for them, and re-layouts, body(): own_weight[None]  26.1 us
    reduce_sum x1, other arithmetic, body(): denominator = jnp.sum(mass_parts, axis=0)  25.5 us
  transfers between devices with their start and end apart: 10, of which 4 were waited for; matrix products, arithmetic and copies ran while one was open for 46% of the time, Pallas kernels for 0%

profile of v1, /device:TPU:26, one launch (start us, length us, event | category | flops | bytes accessed | tf_op | source)
XLA Modules:
  0.0 1265.0 jit_solution(4095054187995246616)
XLA Ops:
  0.6 5.2 copy.14
  5.8 4.5 copy.10
  10.3 6.0 all-to-all-start
  16.3 2.0 collective-permute-start.1
  18.3 1.5 collective-permute-start.2
  19.8 1.5 collective-permute-start.3
  21.2 1.5 collective-permute-start.4
  23.1 26.1 %copy.16 = bf16[1,4096,1792]{2,0,1:T(2,128)(2,1)} copy(bf16[1,4096,1792]{2,1,0:T(8,128)(2,1)} %bitcast.38) | data formatting | bytes 29360128 | tf_op jit(solution)/shard_map/broadcast_in_dim;squeeze | solution.py:90
  49.7 147.2 %reduce = bf16[4096,1792]{1,0:T(8,128)(2,1)} reduce(bf16[4096,1,1792]{2,1,0:T(2,128)(2,1)} %bitcast.36, bf16[]{:T(256)} %broadcast.74), dimensions={1}, to_apply=%bitcast.28.reduce_sub_computation | reduce | bytes 29360130
  196.8 11.5 reshape.134
  208.3 1.5 collective-permute-start.5
  209.8 6.0 transpose.12
  215.8 3.1 constant_dynamic-update-slice_fusion.6
  219.0 6.6 collective-permute-done.1
  225.6 5.4 collective-permute-start.6
  230.9 3.1 constant_dynamic-update-slice_fusion.5
  234.1 36.5 %collective-permute-done.2 = bf16[1,256,4096]{2,1,0:T(8,128)(2,1)} collective-permute-done((bf16[1,256,4096]{2,1,0:T(8,128)(2,1)S(1)}, bf16[1,256,4096]{2,1,0:T(8,128)(2,1)}, u32[]{:S(2)}, u32[]{:S(2)}) %collective-permute-start.2) | collective-permute-done | bytes 2097184 | tf_op jit(solution)/shard_map/ppermute | solution.py:31
  270.5 3.2 constant_dynamic-update-slice_fusion.4
  273.7 260.5 %collective-permute-done.3 = bf16[1,256,4096]{2,1,0:T(8,128)(2,1)} collective-permute-done((bf16[1,256,4096]{2,1,0:T(8,128)(2,1)S(1)}, bf16[1,256,4096]{2,1,0:T(8,128)(2,1)}, u32[]{:S(2)}, u32[]{:S(2)}) %collective-permute-start.3) | collective-permute-done | bytes 2097184 | tf_op jit(solution)/shard_map/ppermute | solution.py:31
  534.2 3.1 constant_dynamic-update-slice_fusion.3
  537.3 3.2 constant_dynamic-update-slice_fusion.2
  540.5 1.4 constant_dynamic-update-slice_fusion.1
  542.0 1.5 constant_dynamic-update-slice_fusion
  543.4 36.5 %gather_fusion = bf16[2048,4096]{1,0:T(8,128)(2,1)} fusion(bf16[2048,4096]{1,0:T(8,128)(2,1)} %bitcast.4, s32[2048]{0:T(1024)S(1)} %broadcast_clamp_fusion), kind=kCustom, calls=%fused_computation | custom fusion | bytes 33562624 | tf_op jit(solution)/shard_map/gather | solution.py:78
  580.0 17.5 %concatenate.6 = bf16[2432,4096]{1,0:T(8,128)(2,1)} pad(bf16[2048,4096]{1,0:T(8,128)(2,1)} %gather_fusion, bf16[]{:T(256)} %constant.143.clone.1), padding=0_384x0_0 | pad | bytes 36700160 | tf_op jit(solution)/shard_map/concatenate | solution.py:43
  597.5 6.7 all-to-all-start.2
  604.2 7.1 concatenate.7
  611.3 220.9 %while.14 = (s32[]{:T(128)}, f32[4096,1792]{1,0:T(8,128)}, s32[8]{0:T(128)S(1)}, s32[8]{0:T(128)S(1)}, bf16[2432,4096]{1,0:T(8,128)(2,1)}, /*index=5*/bf16[2432,1792]{1,0:T(8,128)(2,1)}, s32[]{:T(128)}, s32[]{:T(128)}, s32[]{:T(128)}) while((s32[]{:T(128)}, f32[4096,1792]{1,0:T(8,128)}, s32[8]{0:T(128)S(1)}, s32[8]{0:T(128)S(1)}, ...), condition=%wide.region_2.3_spmd.clone, body=%wide.region_1.2_spmd.clone.sunk | while | flops 5660738048 | bytes 63244708 | solution.py:63
  615.1 15.1 %select_add_fusion.2 = f32[4096,1792]{1,0:T(8,128)} fusion(f32[4096,1792]{1,0:T(8,128)} %get-tuple-element.213, pred[]{:T(512)S(6)} %compare.12, bf16[2432,4096]{1,0:T(8,128)(2,1)} %get-tuple-element.225, s32[]{:T(128)S(6)} %select_n.129, pred[384]{0:T(512)(128)(4,1)S(1)} %iota_compare_fusion.2, bf16[2432,1792]{1,0:T(8,128)(2,1)} %get-tuple-element.226), kind=kOutput, calls=%fused_computation.2.clone.1 | convolution fusion | flops 5660737536 | bytes 63244160 | tf_op jit(solution)/shard_map/while/body/eval_jaxpr/dot_general | solution.py:57
  633.9 25.1 %select_add_fusion.2 = f32[4096,1792]{1,0:T(8,128)} fusion(f32[4096,1792]{1,0:T(8,128)} %get-tuple-element.213, pred[]{:T(512)S(6)} %compare.12, bf16[2432,4096]{1,0:T(8,128)(2,1)} %get-tuple-element.225, s32[]{:T(128)S(6)} %select_n.129, pred[384]{0:T(512)(128)(4,1)S(1)} %iota_compare_fusion.2, bf16[2432,1792]{1,0:T(8,128)(2,1)} %get-tuple-element.226), kind=kOutput, calls=%fused_computation.2.clone.1 | convolution fusion | flops 5660737536 | bytes 63244160 | tf_op jit(solution)/shard_map/while/body/eval_jaxpr/dot_general | solution.py:57
  662.1 0.6 iota_compare_fusion.2
  662.8 25.1 %select_add_fusion.2 = f32[4096,1792]{1,0:T(8,128)} fusion(f32[4096,1792]{1,0:T(8,128)} %get-tuple-element.213, pred[]{:T(512)S(6)} %compare.12, bf16[2432,4096]{1,0:T(8,128)(2,1)} %get-tuple-element.225, s32[]{:T(128)S(6)} %select_n.129, pred[384]{0:T(512)(128)(4,1)S(1)} %iota_compare_fusion.2, bf16[2432,1792]{1,0:T(8,128)(2,1)} %get-tuple-element.226), kind=kOutput, calls=%fused_computation.2.clone.1 | convolution fusion | flops 5660737536 | bytes 63244160 | tf_op jit(solution)/shard_map/while/body/eval_jaxpr/dot_general | solution.py:57
  691.7 25.1 %select_add_fusion.2 = f32[4096,1792]{1,0:T(8,128)} fusion(f32[4096,1792]{1,0:T(8,128)} %get-tuple-element.213, pred[]{:T(512)S(6)} %compare.12, bf16[2432,4096]{1,0:T(8,128)(2,1)} %get-tuple-element.225, s32[]{:T(128)S(6)} %select_n.129, pred[384]{0:T(512)(128)(4,1)S(1)} %iota_compare_fusion.2, bf16[2432,1792]{1,0:T(8,128)(2,1)} %get-tuple-element.226), kind=kOutput, calls=%fused_computation.2.clone.1 | convolution fusion | flops 5660737536 | bytes 63244160 | tf_op jit(solution)/shard_map/while/body/eval_jaxpr/dot_general | solution.py:57
  719.9 0.6 iota_compare_fusion.2
  720.5 25.1 %select_add_fusion.2 = f32[4096,1792]{1,0:T(8,128)} fusion(f32[4096,1792]{1,0:T(8,128)} %get-tuple-element.213, pred[]{:T(512)S(6)} %compare.12, bf16[2432,4096]{1,0:T(8,128)(2,1)} %get-tuple-element.225, s32[]{:T(128)S(6)} %select_n.129, pred[384]{0:T(512)(128)(4,1)S(1)} %iota_compare_fusion.2, bf16[2432,1792]{1,0:T(8,128)(2,1)} %get-tuple-element.226), kind=kOutput, calls=%fused_computation.2.clone.1 | convolution fusion | flops 5660737536 | bytes 63244160 | tf_op jit(solution)/shard_map/while/body/eval_jaxpr/dot_general | solution.py:57
  749.4 25.1 %select_add_fusion.2 = f32[4096,1792]{1,0:T(8,128)} fusion(f32[4096,1792]{1,0:T(8,128)} %get-tuple-element.213, pred[]{:T(512)S(6)} %compare.12, bf16[2432,4096]{1,0:T(8,128)(2,1)} %get-tuple-element.225, s32[]{:T(128)S(6)} %select_n.129, pred[384]{0:T(512)(128)(4,1)S(1)} %iota_compare_fusion.2, bf16[2432,1792]{1,0:T(8,128)(2,1)} %get-tuple-element.226), kind=kOutput, calls=%fused_computation.2.clone.1 | convolution fusion | flops 5660737536 | bytes 63244160 | tf_op jit(solution)/shard_map/while/body/eval_jaxpr/dot_general | solution.py:57
  778.2 25.1 %select_add_fusion.2 = f32[4096,1792]{1,0:T(8,128)} fusion(f32[4096,1792]{1,0:T(8,128)} %get-tuple-element.213, pred[]{:T(512)S(6)} %compare.12, bf16[2432,4096]{1,0:T(8,128)(2,1)} %get-tuple-element.225, s32[]{:T(128)S(6)} %select_n.129, pred[384]{0:T(512)(128)(4,1)S(1)} %iota_compare_fusion.2, bf16[2432,1792]{1,0:T(8,128)(2,1)} %get-tuple-element.226), kind=kOutput, calls=%fused_computation.2.clone.1 | convolution fusion | flops 5660737536 | bytes 63244160 | tf_op jit(solution)/shard_map/while/body/eval_jaxpr/dot_general | solution.py:57
  806.4 0.6 iota_compare_fusion.2
  807.1 25.1 %select_add_fusion.2 = f32[4096,1792]{1,0:T(8,128)} fusion(f32[4096,1792]{1,0:T(8,128)} %get-tuple-element.213, pred[]{:T(512)S(6)} %compare.12, bf16[2432,4096]{1,0:T(8,128)(2,1)} %get-tuple-element.225, s32[]{:T(128)S(6)} %select_n.129, pred[384]{0:T(512)(128)(4,1)S(1)} %iota_compare_fusion.2, bf16[2432,1792]{1,0:T(8,128)(2,1)} %get-tuple-element.226), kind=kOutput, calls=%fused_computation.2.clone.1 | convolution fusion | flops 5660737536 | bytes 63244160 | tf_op jit(solution)/shard_map/while/body/eval_jaxpr/dot_general | solution.py:57
  832.2 21.7 %broadcast_add_fusion = f32[4096,1792]{1,0:T(8,128)} fusion(f32[4096,1792]{1,0:T(8,128)} %get-tuple-element.126), kind=kLoop, calls=%fused_computation.12 | loop fusion | flops 7340032 | bytes 58720256 | tf_op jit(solution)/shard_map/add | solution.py:87
  853.9 24.0 %broadcast_in_dim.38 = f32[1,4096,1792]{2,0,1:T(1,128)} reshape(f32[4096,1792]{1,0:T(8,128)} %broadcast_add_fusion) | data formatting | bytes 58720256 | tf_op jit(solution)/shard_map/broadcast_in_dim | solution.py:91
  877.8 9.4 all-to-all-start.1
  887.3 32.2 %reshape.135 = bf16[4096,1,1792]{2,1,0:T(2,128)(2,1)} reshape(bf16[4,2,917504]{2,1,0:T(2,128)(2,1)} %all-to-all-done.2) | data formatting | bytes 29360128
  919.4 23.8 %copy.13 = f32[1,4096,1792]{2,1,0:T(8,128)} copy(bf16[1,4096,1792]{2,0,1:T(2,128)(2,1)} %bitcast.35) | data formatting | bytes 44040192
  943.3 261.7 %all-to-all-done.1 = f32[1,4096,1792]{2,0,1:T(1,128)} async-done(((f32[1,4096,1792]{2,0,1:T(1,128)}), f32[1,4096,1792]{2,0,1:T(1,128)}, u32[]{:S(2)}, u32[]{:S(2)}) %all-to-all-start.1) | async-done | bytes 29360160 | tf_op jit(solution)/shard_map/all_to_all | solution.py:91
  1205.0 23.8 %copy.12 = f32[1,4096,1792]{2,1,0:T(8,128)} copy(f32[1,4096,1792]{2,0,1:T(1,128)} %all-to-all-done.1) | data formatting | bytes 58720256
  1228.8 25.5 %fusion.10 = (f32[1024,1792]{1,0:T(8,128)}, f32[1024,1792]{1,0:T(8,128)}) fusion(f32[4,1024,1792]{2,1,0:T(8,128)} %bitcast.34, f32[4,1024,1792]{2,1,0:T(8,128)} %bitcast.33), kind=kLoop, calls=%fused_computation.26 | loop fusion | flops 18350080 | bytes 73400320 | tf_op jit(solution)/shard_map/reduce_sum | solution.py:93
  1254.3 10.7 multiply_bitcast_fusion
  (40 shorter events, 13.4 us)
Async XLA Ops:
  5.8 10.5 copy-start
  5.8 16.9 %copy-start.1 = (s32[1,2048]{1,0:T(1,128)S(1)}, s32[1,2048]{1,0:T(1,128)}, u32[]{:S(2)}) copy-start(s32[1,2048]{1,0:T(1,128)} %param.8) | copy-start | bytes 24580
  5.8 16.9 %copy-start.2 = (s32[1,8]{1,0:T(1,128)S(1)}, s32[1,8]{1,0:T(1,128)}, u32[]{:S(2)}) copy-start(s32[1,8]{1,0:T(1,128)} %param.9) | copy-start | bytes 100
  10.3 587.2 %all-to-all-start = ((bf16[256,8,1792]{2,0,1:T(8,128)(2,1)}), bf16[256,8,1792]{2,0,1:T(8,128)(2,1)}, u32[]{:S(2)}, u32[]{:S(2)}) async-start(bf16[256,8,1792]{2,0,1:T(8,128)(2,1)} %copy.10), calls=%async_computation | async-start | bytes 14680064 | tf_op jit(solution)/shard_map/all_to_all | solution.py:85
  16.3 192.1 %collective-permute-start = (bf16[1,256,4096]{2,1,0:T(8,128)(2,1)S(1)}, bf16[1,256,4096]{2,1,0:T(8,128)(2,1)}, u32[]{:S(2)}, u32[]{:S(2)}) collective-permute-start(bf16[1,256,4096]{2,1,0:T(8,128)(2,1)S(1)} %copy-done), channel_id=1, source_target_pairs={{0,4},{4,8},{8,12},{12,16},{16,20},{20,24},{24,28},{28,0},{1,5},{5... | collective-permute-start | bytes 6291464 | tf_op jit(solution)/shard_map/ppermute | solution.py:31
  16.3 209.2 %collective-permute-start.1 = (bf16[1,256,4096]{2,1,0:T(8,128)(2,1)S(1)}, bf16[1,256,4096]{2,1,0:T(8,128)(2,1)}, u32[]{:S(2)}, u32[]{:S(2)}) collective-permute-start(bf16[1,256,4096]{2,1,0:T(8,128)(2,1)S(1)} %copy-done), channel_id=1, source_target_pairs={{0,8},{4,12},{8,16},{12,20},{16,24},{20,28},{24,0},{28,4},{1,9},{5... | collective-permute-start | bytes 6291464 | tf_op jit(solution)/shard_map/ppermute | solution.py:31
  18.3 252.2 %collective-permute-start.2 = (bf16[1,256,4096]{2,1,0:T(8,128)(2,1)S(1)}, bf16[1,256,4096]{2,1,0:T(8,128)(2,1)}, u32[]{:S(2)}, u32[]{:S(2)}) collective-permute-start(bf16[1,256,4096]{2,1,0:T(8,128)(2,1)S(1)} %copy-done), channel_id=1, source_target_pairs={{0,12},{4,16},{8,20},{12,24},{16,28},{20,0},{24,4},{28,8},{1,13},{... | collective-permute-start | bytes 6291464 | tf_op jit(solution)/shard_map/ppermute | solution.py:31
  19.8 514.4 %collective-permute-start.3 = (bf16[1,256,4096]{2,1,0:T(8,128)(2,1)S(1)}, bf16[1,256,4096]{2,1,0:T(8,128)(2,1)}, u32[]{:S(2)}, u32[]{:S(2)}) collective-permute-start(bf16[1,256,4096]{2,1,0:T(8,128)(2,1)S(1)} %copy-done), channel_id=1, source_target_pairs={{0,16},{4,20},{8,24},{12,28},{16,0},{20,4},{24,8},{28,12},{1,17},{... | collective-permute-start | bytes 6291464 | tf_op jit(solution)/shard_map/ppermute | solution.py:31
  21.2 516.1 %collective-permute-start.4 = (bf16[1,256,4096]{2,1,0:T(8,128)(2,1)S(1)}, bf16[1,256,4096]{2,1,0:T(8,128)(2,1)}, u32[]{:S(2)}, u32[]{:S(2)}) collective-permute-start(bf16[1,256,4096]{2,1,0:T(8,128)(2,1)S(1)} %copy-done), channel_id=1, source_target_pairs={{0,20},{4,24},{8,28},{12,0},{16,4},{20,8},{24,12},{28,16},{1,21},{... | collective-permute-start | bytes 6291464 | tf_op jit(solution)/shard_map/ppermute | solution.py:31
  208.3 332.2 %collective-permute-start.5 = (bf16[1,256,4096]{2,1,0:T(8,128)(2,1)S(1)}, bf16[1,256,4096]{2,1,0:T(8,128)(2,1)S(1)}, u32[]{:S(2)}, u32[]{:S(2)}) collective-permute-start(bf16[1,256,4096]{2,1,0:T(8,128)(2,1)S(1)} %copy-done), channel_id=1, source_target_pairs={{0,24},{4,28},{8,0},{12,4},{16,8},{20,12},{24,16},{28,20},{1,25},{... | collective-permute-start | bytes 6291464 | tf_op jit(solution)/shard_map/ppermute | solution.py:31
  225.6 316.4 %collective-permute-start.6 = (bf16[1,256,4096]{2,1,0:T(8,128)(2,1)S(1)}, bf16[1,256,4096]{2,1,0:T(8,128)(2,1)S(1)}, u32[]{:S(2)}, u32[]{:S(2)}) collective-permute-start(bf16[1,256,4096]{2,1,0:T(8,128)(2,1)S(1)} %copy-done), channel_id=1, source_target_pairs={{0,28},{4,0},{8,4},{12,8},{16,12},{20,16},{24,20},{28,24},{1,29},{... | collective-permute-start | bytes 6291464 | tf_op jit(solution)/shard_map/ppermute | solution.py:31
  597.5 280.4 %all-to-all-start.2 = ((bf16[4,2,917504]{2,1,0:T(2,128)(2,1)}), bf16[4,2,917504]{2,1,0:T(2,128)(2,1)}, u32[]{:S(2)}, u32[]{:S(2)}) async-start(bf16[4,2,917504]{2,1,0:T(2,128)(2,1)} %reshape.134), calls=%async_computation.2 | async-start | bytes 29360128 | tf_op jit(solution)/shard_map/all_to_all | solution.py:90
  877.8 327.1 %all-to-all-start.1 = ((f32[1,4096,1792]{2,0,1:T(1,128)}), f32[1,4096,1792]{2,0,1:T(1,128)}, u32[]{:S(2)}, u32[]{:S(2)}) async-start(f32[1,4096,1792]{2,0,1:T(1,128)} %broadcast_in_dim.38), calls=%async_computation.1 | async-start | bytes 58720256 | tf_op jit(solution)/shard_map/all_to_all | solution.py:91
